TPU v7x, 32 devices: a whole 2x2x4 slice. The times are simulated.
32 devices in a mesh: row: 2 (over x), col: 16 (over z, y, core).
Axes of the slice: x: 2, y: 2, z: 4, core: 2. Of those that a mesh axis runs over, the one named last changes fastest.
Arguments:
- tokens: bfloat16 [4096, 1024], P(('row', 'col')), may hold values from -6 to 6
- variate_ids: int32 [4096], P(('row', 'col')), may hold values from 0 to 3
- time_ids: int32 [4096], P(('row', 'col')), may hold values from 0 to 1023
- lengths: int32 [2, 6], P('row'), may hold values from 1 to 8, 16 in all within a row
- deal: int32 [2, 16, 16], P('row', 'col'), may hold values from 0 to 15, each once within a row
- w_qkv: bfloat16 [1024, 3072], P(('row', 'col')), may hold values from -0.1875 to 0.1875
- w_out: bfloat16 [1024, 1024], P(('row', 'col')), may hold values from -3 to 3
- w_gate_up: bfloat16 [1024, 8192], P(('row', 'col')), may hold values from -0.1875 to 0.1875
- w_down: bfloat16 [4096, 1024], P(('row', 'col')), may hold values from -0.09375 to 0.09375
- gain_attn: bfloat16 [1024], P(('row', 'col')), may hold values from 0.5 to 1.5
- gain_ffn: bfloat16 [1024], P(('row', 'col')), may hold values from 0.5 to 1.5
- var_bias: float32 [2, 16], replicated, may hold values from -3 to 3
- cotangent: bfloat16 [4096, 1024], P(('row', 'col')), may hold values from -6 to 6
Outputs:
- output: bfloat16 [4096, 1024], P(('row', 'col'))
- grad_tokens: bfloat16 [4096, 1024], P(('row', 'col'))
- grad_w_qkv: float32 [1024, 3072], P(('row', 'col'))
- grad_w_out: float32 [1024, 1024], P(('row', 'col'))
- grad_w_gate_up: float32 [1024, 8192], P(('row', 'col'))
- grad_w_down: float32 [4096, 1024], P(('row', 'col'))
- grad_gain_attn: float32 [1024], P(('row', 'col'))
- grad_gain_ffn: float32 [1024], P(('row', 'col'))
- grad_var_bias: float32 [2, 16], replicated
All inputs are finite; a program needn't handle non-finite values.
Results may differ from a plain program's by a relative error of at most 0.018.
The roundings to bfloat16 on the way count: a program that leaves them out, or rounds other values in their place, can miss the bound.
Values may be sent and summed in bfloat16 or wider, within the bound.
A program may use at most 320 MiB of HBM per device.

v0:
```python
import math
import jax
import jax.numpy as jnp
from jax import lax
from jax.sharding import PartitionSpec as P

HEAD_DIM = 64
UNIT = 128
KEY_BLOCK = 1024
epsilon = 1e-05


def contract_rows(operand, factor):
    return lax.dot_general(
        operand, factor, (((0,), (0,)), ((), ())), preferred_element_type=jnp.float32
    )


def contract_cols(operand, factor):
    return lax.dot_general(
        operand, factor, (((1,), (1,)), ((), ())), preferred_element_type=jnp.float32
    )


def angles(time_ids):
    half_dim = HEAD_DIM // 2
    inverse_freq = jnp.exp(-math.log(10000.0) * jnp.arange(half_dim, dtype=jnp.float32) / half_dim)
    phases = time_ids.astype(jnp.float32)[:, None] * inverse_freq[None, :]
    return (jnp.cos(phases)[:, None, :], jnp.sin(phases)[:, None, :])


def rotate(tensor, cos_part, sin_part):
    half_dim = tensor.shape[-1] // 2
    former = tensor[..., :half_dim]
    latter = tensor[..., half_dim:]
    return jnp.concatenate(
        [former * cos_part - latter * sin_part, latter * cos_part + former * sin_part], axis=-1
    )


def unrotate(tensor, cos_part, sin_part):
    half_dim = tensor.shape[-1] // 2
    former = tensor[..., :half_dim]
    latter = tensor[..., half_dim:]
    return jnp.concatenate(
        [former * cos_part + latter * sin_part, latter * cos_part - former * sin_part], axis=-1
    )


def norm_scale(values):
    return lax.rsqrt(jnp.mean(values * values, axis=-1, keepdims=True) + epsilon)


def norm_back(d_normed, normed, scale):
    return scale * (d_normed - normed * jnp.mean(d_normed * normed, axis=-1, keepdims=True))


def score_weights(queries, query_seq, query_var, key_block, seq_block, var_block, var_bias):
    scores = (
        jnp.einsum("qhd,khd->hqk", queries, key_block, preferred_element_type=jnp.float32) * 0.125
    )
    matched = query_var[:, None] == var_block[None, :]
    scores = scores + jnp.where(
        matched[None], var_bias[0][:, None, None], var_bias[1][:, None, None]
    )
    within = query_seq[:, None] == seq_block[None, :]
    return (jnp.where(within[None], jnp.exp(scores), 0.0), matched)


def shards(
    tokens,
    variate_ids,
    time_ids,
    lengths,
    deal,
    w_qkv,
    w_out,
    w_gate_up,
    w_down,
    gain_attn,
    gain_ffn,
    var_bias,
    cotangent,
):
    tok_rows, model_width = tokens.shape
    n_col = lax.axis_size("col")
    col_index = lax.axis_index("col")
    piece_len = tok_rows // n_col
    head_count = model_width // HEAD_DIM
    bounds = jnp.cumsum(lengths[0]) * UNIT
    position = col_index * tok_rows + jnp.arange(tok_rows, dtype=jnp.int32)
    seq_own = jnp.sum((position[:, None] >= bounds[None, :]).astype(jnp.int32), axis=1)
    target = deal[0, 0]
    slots = jnp.arange(n_col, dtype=jnp.int32)
    inverse = jnp.sum(
        slots[:, None] * (target[:, None] == slots[None, :]).astype(jnp.int32), axis=0
    )
    send_rows = jnp.take(tokens.reshape(n_col, piece_len, model_width), inverse, axis=0)
    labels = jnp.stack(
        [
            seq_own.reshape(n_col, piece_len),
            variate_ids.reshape(n_col, piece_len),
            time_ids.reshape(n_col, piece_len),
        ],
        axis=1,
    )
    send_labels = jnp.take(labels, inverse, axis=0)
    got_rows, got_labels = (
        lax.all_to_all(send_rows, "col", split_axis=0, concat_axis=0, tiled=True),
        lax.all_to_all(send_labels, "col", split_axis=0, concat_axis=0, tiled=True),
    )
    inputs = got_rows.reshape(tok_rows, model_width).astype(jnp.float32)
    seq_q = got_labels[:, 0, :].reshape(tok_rows)
    var_q = got_labels[:, 1, :].reshape(tok_rows)
    cos_part, sin_part = angles(got_labels[:, 2, :].reshape(tok_rows))
    qkv_full, out_full, gate_up_full, down_full, gain_one, gain_two = (
        lax.all_gather(w_qkv, ("row", "col"), axis=0, tiled=True),
        lax.all_gather(w_out, ("row", "col"), axis=0, tiled=True),
        lax.all_gather(w_gate_up, ("row", "col"), axis=0, tiled=True),
        lax.all_gather(w_down, ("row", "col"), axis=0, tiled=True),
        lax.all_gather(gain_attn, ("row", "col"), axis=0, tiled=True),
        lax.all_gather(gain_ffn, ("row", "col"), axis=0, tiled=True),
    )
    scale_one = norm_scale(inputs)
    normed_one = inputs * scale_one
    scaled_one = (normed_one * gain_one.astype(jnp.float32)).astype(jnp.bfloat16)
    projected = jnp.dot(scaled_one, qkv_full, preferred_element_type=jnp.float32)
    shaped = projected.reshape(tok_rows, 3, head_count, HEAD_DIM)
    queries = rotate(shaped[:, 0], cos_part, sin_part).astype(jnp.bfloat16)
    key_own = (
        rotate(shaped[:, 1], cos_part, sin_part).astype(jnp.bfloat16).reshape(tok_rows, model_width)
    )
    value_own = projected[:, 2 * model_width :].astype(jnp.bfloat16)
    keys_all, values_all, seq_k, var_k = (
        lax.all_gather(key_own, "col", axis=0, tiled=True),
        lax.all_gather(value_own, "col", axis=0, tiled=True),
        lax.all_gather(seq_q, "col", axis=0, tiled=True),
        lax.all_gather(var_q, "col", axis=0, tiled=True),
    )
    group_size = keys_all.shape[0]
    stride = min(KEY_BLOCK, group_size)
    block_count = group_size // stride

    def split_blocks(key_rows, value_rows, key_seq, key_var):
        return (
            key_rows.reshape(block_count, stride, head_count, HEAD_DIM),
            value_rows.reshape(block_count, stride, head_count, HEAD_DIM),
            key_seq.reshape(block_count, stride),
            key_var.reshape(block_count, stride),
        )

    def forward_step(running, block_data):
        denominator, numerator = running
        key_block, value_block, seq_block, var_block = block_data
        weights = score_weights(queries, seq_q, var_q, key_block, seq_block, var_block, var_bias)[0]
        denominator = denominator + jnp.sum(weights, axis=-1)
        numerator = numerator + jnp.einsum(
            "hqk,khd->qhd",
            weights.astype(jnp.bfloat16),
            value_block,
            preferred_element_type=jnp.float32,
        )
        return ((denominator, numerator), None)

    (denominator, numerator), unused = lax.scan(
        forward_step,
        (
            jnp.zeros((head_count, tok_rows), jnp.float32),
            jnp.zeros((tok_rows, head_count, HEAD_DIM), jnp.float32),
        ),
        split_blocks(keys_all, values_all, seq_k, var_k),
    )
    attended = numerator / denominator.T[:, :, None]
    attn_low = attended.reshape(tok_rows, model_width).astype(jnp.bfloat16)
    hidden_state = inputs + jnp.dot(attn_low, out_full, preferred_element_type=jnp.float32)
    scale_two = norm_scale(hidden_state)
    normed_two = hidden_state * scale_two
    scaled_two = (normed_two * gain_two.astype(jnp.float32)).astype(jnp.bfloat16)
    gate_up = jnp.dot(scaled_two, gate_up_full, preferred_element_type=jnp.float32)
    hidden_units = gate_up_full.shape[1] // 2
    gate_part = gate_up[:, :hidden_units]
    upper_part = gate_up[:, hidden_units:]
    sigmoid_gate = jax.nn.sigmoid(gate_part)
    active = gate_part * sigmoid_gate
    inner_act = (active * upper_part).astype(jnp.bfloat16)
    ffn_branch = jnp.dot(inner_act, down_full, preferred_element_type=jnp.float32)
    output = (hidden_state + ffn_branch).astype(jnp.bfloat16)
    qkv_back, out_back, gate_up_back, down_back, gain_one_back, gain_two_back = (
        lax.all_gather(w_qkv, ("row", "col"), axis=0, tiled=True),
        lax.all_gather(w_out, ("row", "col"), axis=0, tiled=True),
        lax.all_gather(w_gate_up, ("row", "col"), axis=0, tiled=True),
        lax.all_gather(w_down, ("row", "col"), axis=0, tiled=True),
        lax.all_gather(gain_attn, ("row", "col"), axis=0, tiled=True),
        lax.all_gather(gain_ffn, ("row", "col"), axis=0, tiled=True),
    )
    d_inner = contract_cols(cotangent, down_back)
    d_gate = (
        d_inner * upper_part * sigmoid_gate * (1.0 + gate_part * (1.0 - sigmoid_gate))
    ).astype(jnp.bfloat16)
    d_upper = (d_inner * active).astype(jnp.bfloat16)
    d_gate_up = jnp.concatenate([d_gate, d_upper], axis=1)
    d_scaled_two = contract_cols(d_gate_up, gate_up_back)
    term_gain_two = jnp.sum(d_scaled_two * normed_two, axis=0)
    term_gate_up = contract_rows(scaled_two, d_gate_up)
    term_down = contract_rows(inner_act, cotangent)
    d_hidden = cotangent.astype(jnp.float32) + norm_back(
        d_scaled_two * gain_two_back.astype(jnp.float32), normed_two, scale_two
    )
    d_branch = d_hidden.astype(jnp.bfloat16)
    term_out = contract_rows(attn_low, d_branch)
    d_attended = contract_cols(d_branch, out_back).reshape(tok_rows, head_count, HEAD_DIM)
    d_numerator = (d_attended / denominator.T[:, :, None]).astype(jnp.bfloat16)
    centre = (jnp.sum(d_attended * attended, axis=-1) / denominator.T).T
    back_keys = (
        lax.all_gather(key_own, "col", axis=0, tiled=True),
        lax.all_gather(value_own, "col", axis=0, tiled=True),
        lax.all_gather(seq_q, "col", axis=0, tiled=True),
        lax.all_gather(var_q, "col", axis=0, tiled=True),
    )

    def query_step(running, block_data):
        d_queries, same_sum, other_sum = running
        key_block, value_block, seq_block, var_block = block_data
        weights, matched = score_weights(
            queries, seq_q, var_q, key_block, seq_block, var_block, var_bias
        )
        d_probs = jnp.einsum(
            "qhd,khd->hqk", d_numerator, value_block, preferred_element_type=jnp.float32
        )
        d_scores = weights * (d_probs - centre[:, :, None])
        same_sum = same_sum + jnp.sum(jnp.where(matched[None], d_scores, 0.0), axis=(1, 2))
        other_sum = other_sum + jnp.sum(jnp.where(matched[None], 0.0, d_scores), axis=(1, 2))
        d_rounded = d_scores.astype(jnp.bfloat16)
        d_queries = d_queries + jnp.einsum(
            "hqk,khd->qhd", d_rounded, key_block, preferred_element_type=jnp.float32
        )
        return ((d_queries, same_sum, other_sum), (d_rounded, weights.astype(jnp.bfloat16)))

    def query_and_key_step(running, block_data):
        running, rounded = query_step(running, block_data)
        d_rounded, weights_low = rounded
        d_keys = (
            jnp.einsum("hqk,qhd->khd", d_rounded, queries, preferred_element_type=jnp.float32)
            * 0.125
        )
        d_values = jnp.einsum(
            "hqk,qhd->khd", weights_low, d_numerator, preferred_element_type=jnp.float32
        )
        return (running, (d_keys, d_values))

    start_running = (
        jnp.zeros((tok_rows, head_count, HEAD_DIM), jnp.float32),
        jnp.zeros((head_count,), jnp.float32),
        jnp.zeros((head_count,), jnp.float32),
    )
    (d_queries, same_sum, other_sum), (d_keys, d_values) = lax.scan(
        query_and_key_step,
        start_running,
        split_blocks(back_keys[0], back_keys[1], back_keys[2], back_keys[3]),
    )
    key_grad, value_grad = (
        lax.psum_scatter(
            d_keys.reshape(group_size, model_width).astype(jnp.bfloat16),
            "col",
            scatter_dimension=0,
            tiled=True,
        ).astype(jnp.float32),
        lax.psum_scatter(
            d_values.reshape(group_size, model_width).astype(jnp.bfloat16),
            "col",
            scatter_dimension=0,
            tiled=True,
        ).astype(jnp.float32),
    )
    d_query_pre = unrotate(d_queries * 0.125, cos_part, sin_part).reshape(tok_rows, model_width)
    d_key_pre = unrotate(
        key_grad.reshape(tok_rows, head_count, HEAD_DIM), cos_part, sin_part
    ).reshape(tok_rows, model_width)
    d_projected = jnp.concatenate([d_query_pre, d_key_pre, value_grad], axis=1).astype(jnp.bfloat16)
    d_scaled_one = contract_cols(d_projected, qkv_back)
    term_qkv = contract_rows(scaled_one, d_projected)
    term_gain_one = jnp.sum(d_scaled_one * normed_one, axis=0)
    grad_w_qkv, grad_w_out, grad_w_gate_up, grad_w_down, grad_gain_attn, grad_gain_ffn = (
        lax.psum_scatter(term_qkv, ("row", "col"), scatter_dimension=0, tiled=True),
        lax.psum_scatter(term_out, ("row", "col"), scatter_dimension=0, tiled=True),
        lax.psum_scatter(term_gate_up, ("row", "col"), scatter_dimension=0, tiled=True),
        lax.psum_scatter(term_down, ("row", "col"), scatter_dimension=0, tiled=True),
        lax.psum_scatter(term_gain_one, ("row", "col"), scatter_dimension=0, tiled=True),
        lax.psum_scatter(term_gain_two, ("row", "col"), scatter_dimension=0, tiled=True),
    )
    grad_var_bias = lax.psum(jnp.stack([same_sum, other_sum], axis=0), ("row", "col"))
    d_inputs = d_hidden + norm_back(
        d_scaled_one * gain_one_back.astype(jnp.float32), normed_one, scale_one
    )
    returned = lax.all_to_all(
        d_inputs.astype(jnp.bfloat16).reshape(n_col, piece_len, model_width),
        "col",
        split_axis=0,
        concat_axis=0,
        tiled=True,
    )
    grad_tokens = jnp.take(returned, target, axis=0).reshape(tok_rows, model_width)
    return (
        output,
        grad_tokens,
        grad_w_qkv,
        grad_w_out,
        grad_w_gate_up,
        grad_w_down,
        grad_gain_attn,
        grad_gain_ffn,
        grad_var_bias,
    )


def solution(mesh):
    return jax.shard_map(
        shards,
        mesh=mesh,
        in_specs=(
            P(("row", "col"), None),
            P(("row", "col")),
            P(("row", "col")),
            P("row", None),
            P("row", "col", None),
            P(("row", "col"), None),
            P(("row", "col"), None),
            P(("row", "col"), None),
            P(("row", "col"), None),
            P(("row", "col")),
            P(("row", "col")),
            P(),
            P(("row", "col"), None),
        ),
        out_specs=(
            P(("row", "col"), None),
            P(("row", "col"), None),
            P(("row", "col"), None),
            P(("row", "col"), None),
            P(("row", "col"), None),
            P(("row", "col"), None),
            P(("row", "col")),
            P(("row", "col")),
            P(),
        ),
        check_vma=False,
    )
```

profile of v0, /device:TPU:1, one launch (start us, length us, event | category | flops | bytes accessed | tf_op | source)
XLA Modules:
  0.0 1548.9 jit_solution(3545822266853017098)
XLA Ops:
  12.5 7.3 all-to-all-start.1
  21.3 4.6 all-to-all-done.1
  25.9 4.1 all-to-all-start
  31.7 41.9 %all-reduce.5 = (bf16[1024]{0:T(1024)(128)(2,1)S(1)}, bf16[1024]{0:T(1024)(128)(2,1)S(1)}) all-reduce(bf16[1024]{0:T(1024)(128)(2,1)S(1)} %dynamic-update-slice, bf16[1024]{0:T(1024)(128)(2,1)S(1)} %dynamic-update-slice.1), channel_id=1, replica_groups=mesh['row'=2,'col'=16] {'row','col'}, use_global_device_ids=true, to_apply=%add | all-reduce | flops 2048 | bytes 8192
  74.2 11.2 all-gather.9.cloned.1.call-done
  85.3 3.8 fusion.91
  89.2 1.6 copy.80
  90.8 1.3 slice_bitcast_fusion.4
  96.3 19.8 %all-gather = s32[16,1,128]{2,1,0:T(1,128)S(1)} all-gather(s32[1,1,128]{2,1,0:T(1,128)S(1)} %reshape.400), channel_id=1, replica_groups=mesh['row'=2,'col'=16] {'col'}, dimensions={0}, use_global_device_ids=true | all-gather | bytes 8704 | tf_op jit(solution)/shard_map/all_gather | solution.py:137
  117.4 17.5 %all-gather.1 = s32[16,1,128]{2,1,0:T(1,128)S(1)} all-gather(s32[1,1,128]{2,1,0:T(1,128)S(1)} %reshape.402), channel_id=1, replica_groups=mesh['row'=2,'col'=16] {'col'}, dimensions={0}, use_global_device_ids=true | all-gather | bytes 8704 | tf_op jit(solution)/shard_map/all_gather | solution.py:138
  135.7 9.3 all-gather.11.cloned.1.call-done
  145.0 7.9 reshape.357
  152.8 5.7 copy.83
  158.5 38.1 %all-gather.13.cloned.1.call-done = bf16[2048,1024]{1,0:T(8,128)(2,1)} async-done(((bf16[128,1024]{1,0:T(8,128)(2,1)}), bf16[2048,1024]{1,0:T(8,128)(2,1)}) %all-gather.13.cloned.1.call-update) | async-done | bytes 4194320 | tf_op jit(solution)/shard_map/all_gather | solution.py:136
  196.7 11.6 reshape.416
  208.3 9.8 copy.85
  218.1 31.7 %while.34 = (s32[]{:T(128)}, f32[16,128]{1,0:T(8,128)S(1)}, f32[128,16,64]{0,2,1:T(8,128)S(1)}, s32[16,1,8]{2,0,1:T(8,128)}, s32[2,1024]{1,0:T(2,128)S(1)}, /*in...) while((s32[]{:T(128)}, f32[16,128]{1,0:T(8,128)S(1)}, ...), condition=%wide.wide.region_6.8_spmd.clone, body=%wide.wide.region_4.7_spmd.clone.sunk | while | flops 558368768 | bytes 23127724 | solution.py:165
  218.5 8.7 fusion.161
  227.2 6.6 fusion.162
  234.2 8.7 fusion.161
  242.9 6.6 fusion.162
  249.8 4.5 all-gather.15.cloned.1.call-done
  254.3 2.1 multiply_reduce_fusion.3
  256.5 114.3 %all-gather.17.cloned.1.call-done = bf16[1024,8192]{1,0:T(8,128)(2,1)} async-done(((bf16[32,8192]{1,0:T(8,128)(2,1)}), bf16[1024,8192]{1,0:T(8,128)(2,1)}) %all-gather.17.cloned.1.call-update) | async-done | bytes 16777232 | tf_op jit(solution)/shard_map/all_gather | solution.py:119
  370.8 10.2 fusion.99
  381.0 68.3 %all-gather.19.cloned.1.call-done = bf16[4096,1024]{1,0:T(8,128)(2,1)} async-done(((bf16[128,1024]{1,0:T(8,128)(2,1)}), bf16[4096,1024]{1,0:T(8,128)(2,1)}) %all-gather.19.cloned.1.call-update) | async-done | bytes 8388624 | tf_op jit(solution)/shard_map/all_gather | solution.py:120
  449.3 9.1 multiply_convert_fusion.1
  458.5 13.5 multiply_reduce_fusion
  472.0 1.3 multiply_add_fusion
  473.3 2.3 fusion.88
  476.4 46.5 %while.35 = (s32[]{:T(128)}, f32[128,16,64]{0,2,1:T(8,128)S(1)}, f32[16]{0:T(128)S(1)}, f32[16]{0:T(128)S(1)}, bf16[2,1024,16,64]{1,3,2,0:T(8,128)(2,1)}, /*inde...) while((s32[]{:T(128)}, f32[128,16,64]{0,2,1:T(8,128)S(1)}, ...), condition=%wide.wide.region_13.15_spmd.clone, body=%wide.wide.region_10.14_spmd.clone.sunk | while | flops 1377304576 | bytes 158108944 | solution.py:256
  477.1 3.1 fusion.172
  480.4 7.2 select_reduce_fusion.5
  487.7 3.9 fusion.173
  491.7 2.9 bitcast_dynamic-update-slice_fusion.6
  494.6 1.2 copy-done.4
  495.8 4.1 bitcast_dynamic-update-slice_fusion.7
  500.1 3.1 fusion.172
  503.5 7.2 select_reduce_fusion.5
  510.7 3.9 fusion.173
  514.7 3.0 bitcast_dynamic-update-slice_fusion.6
  517.7 1.2 copy-done.4
  518.9 4.1 bitcast_dynamic-update-slice_fusion.7
  523.0 10.9 copy.104
  533.9 11.9 reshape.412
  545.8 11.2 copy.105
  557.0 12.0 reshape.414
  570.0 2.8 fusion.86
  573.8 41.2 %reduce-scatter.19.cloned.1.call-done = bf16[128,1024]{1,0:T(8,128)(2,1)} async-done(((bf16[2048,1024]{1,0:T(8,128)(2,1)}), bf16[128,1024]{1,0:T(8,128)(2,1)}) %reduce-scatter.19.cloned.1.call-update) | async-done | bytes 262160
  614.9 1.1 copy.99
  616.1 74.7 %reduce-scatter.21.cloned.1.call-done = bf16[128,1024]{1,0:T(8,128)(2,1)} async-done(((bf16[2048,1024]{1,0:T(8,128)(2,1)}), bf16[128,1024]{1,0:T(8,128)(2,1)}) %reduce-scatter.21.cloned.1.call-update) | async-done | bytes 262160
  690.8 1.1 copy.101
  691.9 1.2 add_convert_fusion.1
  693.2 6.4 fusion.82
  700.6 8.1 fusion.100
  708.7 14.9 fusion.66
  724.3 5.1 fusion.80
  730.3 6.0 all-to-all-start.2
  736.3 5.4 fusion.68
  741.7 40.7 %all-reduce.4 = (f32[1024]{0:T(1024)S(1)}, f32[1024]{0:T(1024)S(1)}, f32[2,16]{1,0:T(2,128)}) all-reduce(f32[1024]{0:T(1024)S(1)} %get-tuple-element.360, f32[1024]{0:T(1024)S(1)} %copy-done.25, f32[2,16]{1,0:T(2,128)S(1)} %pad_maximum_fusion.10), channel_id=8, replica_groups=mesh['row'=2,'col'=16] {'row','col'}, use_global_device_ids=true, to_apply=%region_22.24.clone | all-reduce | flops 2080 | bytes 16640
  784.9 45.3 %reduce-scatter.13.cloned.1.call-done = f32[32,1024]{1,0:T(8,128)} async-done(((f32[1024,1024]{1,0:T(8,128)}), f32[32,1024]{1,0:T(8,128)}) %reduce-scatter.13.cloned.1.call-update) | async-done | bytes 131088 | tf_op jit(solution)/shard_map/reduce_scatter | solution.py:285
  830.2 162.6 %reduce-scatter.11.cloned.1.call-done = f32[32,3072]{1,0:T(8,128)} async-done(((f32[1024,3072]{1,0:T(8,128)}), f32[32,3072]{1,0:T(8,128)}) %reduce-scatter.11.cloned.1.call-update) | async-done | bytes 393232 | tf_op jit(solution)/shard_map/reduce_scatter | solution.py:284
  992.8 187.5 %reduce-scatter.17.cloned.1.call-done = f32[128,1024]{1,0:T(8,128)} async-done(((f32[4096,1024]{1,0:T(8,128)}), f32[128,1024]{1,0:T(8,128)}) %reduce-scatter.17.cloned.1.call-update) | async-done | bytes 524304 | tf_op jit(solution)/shard_map/reduce_scatter | solution.py:287
  1180.3 361.5 %reduce-scatter.15.cloned.1.call-done = f32[32,8192]{1,0:T(8,128)} async-done(((f32[1024,8192]{1,0:T(8,128)}), f32[32,8192]{1,0:T(8,128)}) %reduce-scatter.15.cloned.1.call-update) | async-done | bytes 1048592 | tf_op jit(solution)/shard_map/reduce_scatter | solution.py:286
  (184 shorter events, 24.9 us)
Async XLA Ops:
  7.2 12.7 copy-start
  7.2 78.1 %all-gather.9.cloned.1.call-start = ((), (), s32[]{:S(2)}) async-start(), calls=%async_computation.9 | async-start | bytes 6488064 | tf_op jit(solution)/shard_map/all_gather | solution.py:117
  12.5 13.4 all-to-all-start.1
  25.9 48.0 %all-to-all-start = ((bf16[16,8,1024]{2,1,0:T(8,128)(2,1)}), bf16[16,8,1024]{2,1,0:T(8,128)(2,1)S(1)}, u32[]{:S(2)}, u32[]{:S(2)}) async-start(bf16[16,8,1024]{2,1,0:T(8,128)(2,1)} %broadcast_select_fusion.2), calls=%async_computation | async-start | bytes 524288 | tf_op jit(solution)/shard_map/all_to_all | solution.py:109
  29.9 115.0 %all-gather.11.cloned.1.call-start = ((), (), s32[]{:S(2)}) async-start(), calls=%async_computation.10 | async-start | bytes 4456448 | tf_op jit(solution)/shard_map/all_gather | solution.py:135
  73.6 15.6 %copy-start.12 = (f32[1024]{0:T(1024)}, f32[1024]{0:T(1024)S(1)}, u32[]{:S(2)}) copy-start(f32[1024]{0:T(1024)S(1)} %convert_element_type.102) | copy-start | bytes 12292
  73.9 18.2 %copy-start.16 = (f32[128,32]{0,1:T(8,128)}, f32[128,32]{0,1:T(8,128)S(1)}, u32[]{:S(2)}) copy-start(f32[128,32]{0,1:T(8,128)S(1)} %get-tuple-element.455) | copy-start | bytes 49156
  73.9 18.2 %copy-start.18 = (f32[128,32]{0,1:T(8,128)}, f32[128,32]{0,1:T(8,128)S(1)}, u32[]{:S(2)}) copy-start(f32[128,32]{0,1:T(8,128)S(1)} %get-tuple-element.456) | copy-start | bytes 49156
  74.2 15.0 copy-start.23
  93.1 103.6 %all-gather.13.cloned.1.call-start = ((), (), s32[]{:S(2)}) async-start(), calls=%async_computation.11 | async-start | bytes 4456448 | tf_op jit(solution)/shard_map/all_gather | solution.py:136
  93.9 160.5 %all-gather.15.cloned.1.call-start = ((), (), s32[]{:S(2)}) async-start(), calls=%async_computation.12 | async-start | bytes 2162688 | tf_op jit(solution)/shard_map/all_gather | solution.py:118
  94.5 276.4 %all-gather.17.cloned.1.call-start = ((), (), s32[]{:S(2)}) async-start(), calls=%async_computation.13 | async-start | bytes 17301504 | tf_op jit(solution)/shard_map/all_gather | solution.py:119
  95.0 354.3 %all-gather.19.cloned.1.call-start = ((), (), s32[]{:S(2)}) async-start(), calls=%async_computation.14 | async-start | bytes 8650752 | tf_op jit(solution)/shard_map/all_gather | solution.py:120
  95.6 519.3 %reduce-scatter.19.cloned.1.call-start = ((), (), s32[]{:S(2)}) async-start(), calls=%async_computation.19 | async-start | bytes 4456448
  95.8 57.0 %copy-start.21 = (s32[16,1,8]{2,1,0:T(1,128)}, s32[16,1,8]{2,1,0:T(1,128)S(1)}, u32[]{:S(2)}) copy-start(s32[16,1,8]{2,1,0:T(1,128)S(1)} %get-tuple-element.449) | copy-start | bytes 1540
  95.8 57.0 %copy-start.22 = (s32[16,1,8]{2,1,0:T(1,128)}, s32[16,1,8]{2,1,0:T(1,128)S(1)}, u32[]{:S(2)}) copy-start(s32[16,1,8]{2,1,0:T(1,128)S(1)} %get-tuple-element.452) | copy-start | bytes 1540
  208.3 9.8 copy-start.20
  249.7 131.2 %copy-start.8 = (f32[128,16,64]{0,2,1:T(8,128)}, f32[128,16,64]{0,2,1:T(8,128)S(1)}, u32[]{:S(2)}) copy-start(f32[128,16,64]{0,2,1:T(8,128)S(1)} %get-tuple-element.154) | copy-start | bytes 1572868
  249.8 131.2 %copy-start.6 = (bf16[128,16,64]{0,2,1:T(8,128)(2,1)}, bf16[128,16,64]{0,2,1:T(8,128)(2,1)S(1)}, u32[]{:S(2)}) copy-start(bf16[128,16,64]{0,2,1:T(8,128)(2,1)S(1)} %fusion.85) | copy-start | bytes 786436
  370.8 78.5 %copy-start.10 = (bf16[128,1024]{1,0:T(8,128)(2,1)S(1)}, bf16[128,1024]{1,0:T(8,128)(2,1)}, u32[]{:S(2)}) copy-start(bf16[128,1024]{1,0:T(8,128)(2,1)} %param.31) | copy-start | bytes 786436
  472.0 3.6 copy-start.9
  477.1 3.4 copy-start.5
  477.1 3.4 copy-start.14
  480.2 7.5 copy-start.3
  487.7 4.0 copy-start.2
  491.7 4.1 copy-start.4
  491.7 4.1 copy-start.15
  500.1 3.4 copy-start.5
  500.1 3.4 copy-start.14
  503.3 7.5 copy-start.3
  510.7 4.0 copy-start.2
  514.7 4.1 copy-start.4
  514.7 4.1 copy-start.15
  545.8 145.0 %reduce-scatter.21.cloned.1.call-start = ((), (), s32[]{:S(2)}) async-start(), calls=%async_computation.20 | async-start | bytes 4456448
  569.1 0.9 copy-start.7
  569.1 261.1 %reduce-scatter.13.cloned.1.call-start = ((), (), s32[]{:S(2)}) async-start(), calls=%async_computation.16 | async-start | bytes 4325376 | tf_op jit(solution)/shard_map/reduce_scatter | solution.py:285
  572.8 119.1 %copy-start.17 = (f32[128,32]{0,1:T(8,128)S(1)}, f32[128,32]{0,1:T(8,128)}, u32[]{:S(2)}) copy-start(f32[128,32]{0,1:T(8,128)} %copy-done.16) | copy-start | bytes 49156
  572.8 119.1 %copy-start.19 = (f32[128,32]{0,1:T(8,128)S(1)}, f32[128,32]{0,1:T(8,128)}, u32[]{:S(2)}) copy-start(f32[128,32]{0,1:T(8,128)} %copy-done.18) | copy-start | bytes 49156
  572.9 120.3 %copy-start.13 = (f32[1024]{0:T(1024)S(1)}, f32[1024]{0:T(1024)}, u32[]{:S(2)}) copy-start(f32[1024]{0:T(1024)} %copy-done.12) | copy-start | bytes 12292
  572.9 120.4 %copy-start.24 = (f32[128]{0:T(128)S(1)}, f32[128]{0:T(128)}, u32[]{:S(2)}) copy-start(f32[128]{0:T(128)} %copy-done.23) | copy-start | bytes 1540
  572.9 419.9 %reduce-scatter.11.cloned.1.call-start = ((), (), s32[]{:S(2)}) async-start(), calls=%async_computation.15 | async-start | bytes 12976128 | tf_op jit(solution)/shard_map/reduce_scatter | solution.py:284
  699.6 1.0 copy-start.11
  699.6 480.7 %reduce-scatter.17.cloned.1.call-start = ((), (), s32[]{:S(2)}) async-start(), calls=%async_computation.18 | async-start | bytes 17301504 | tf_op jit(solution)/shard_map/reduce_scatter | solution.py:287
  708.7 833.2 %reduce-scatter.15.cloned.1.call-start = ((), (), s32[]{:S(2)}) async-start(), calls=%async_computation.17 | async-start | bytes 34603008 | tf_op jit(solution)/shard_map/reduce_scatter | solution.py:286
  723.6 0.7 copy-start.26
  730.3 53.2 %all-to-all-start.2 = ((bf16[16,8,1024]{2,1,0:T(8,128)(2,1)}), bf16[16,8,1024]{2,1,0:T(8,128)(2,1)S(1)}, u32[]{:S(2)}, u32[]{:S(2)}) async-start(bf16[16,8,1024]{2,1,0:T(8,128)(2,1)} %fusion.84), calls=%async_computation.2 | async-start | bytes 524288 | tf_op jit(solution)/shard_map/all_to_all | solution.py:295
  736.3 5.4 copy-start.25
  736.3 805.5 %copy-start.1 = (bf16[128,1024]{1,0:T(8,128)(2,1)S(1)}, bf16[128,1024]{1,0:T(8,128)(2,1)}, u32[]{:S(2)}) copy-start(bf16[128,1024]{1,0:T(8,128)(2,1)} %param.19) | copy-start | bytes 786436
Sparse Core Ops, SparseCore 0:
  10.9 74.3 all-gather.8
  93.2 51.7 all-gather.10
  147.7 48.8 all-gather.12
  199.4 54.9 all-gather.14
  257.1 113.7 all-gather.16
  373.6 75.7 all-gather.18
  545.9 68.9 reduce-scatter.18
  619.3 71.4 reduce-scatter.20
  693.7 136.5 reduce-scatter.12
  836.7 156.0 reduce-scatter.10
  995.8 184.4 reduce-scatter.16
  1183.1 358.6 reduce-scatter.14
where the time goes:
time: 1560 us; the launch traced here: 1550 us
  waiting for transfers between devices  1130 us (72%)
  matrix products  157 us (10%)
  blocking collectives  120 us (8%)
  local copies, waits for them, and re-layouts  99.4 us (6%)
  starting transfers between devices  17.8 us (1%)
    reduce_scatter x1, waiting for transfers between devices, shards(): lax.psum_scatter(term_gate_up, ('row', 'col'), scatter_dimension=0, tiled...  362 us
    reduce_scatter x1, waiting for transfers between devices, shards(): lax.psum_scatter(term_down, ('row', 'col'), scatter_dimension=0, tiled=True)  187 us
    reduce_scatter x1, waiting for transfers between devices, shards(): lax.psum_scatter(term_qkv, ('row', 'col'), scatter_dimension=0, tiled=True)  163 us
    unnamed x14, waiting for transfers between devices  118 us
    all_gather x1, waiting for transfers between devices, shards(): lax.all_gather(w_gate_up, ('row', 'col'), axis=0, tiled=True)  114 us
    unnamed x2, blocking collectives  82.6 us
    unnamed x58, local copies, waits for them, and re-layouts  69.2 us
    all_gather x1, waiting for transfers between devices, shards(): lax.all_gather(w_down, ('row', 'col'), axis=0, tiled=True)  68.3 us
  transfers between devices with their start and end apart: 15, of which 13 were waited for; matrix products, arithmetic and copies ran while one was open for 11% of the time, Pallas kernels for 0%

commit v1 on v0

--- a/solution.py
+++ b/solution.py
@@ -8,6 +8,24 @@
 UNIT = 128
 KEY_BLOCK = 1024
 epsilon = 1e-05
+
+
+def gather_around(shard, axis, dim):
+    ways, here, lap = (lax.axis_size(axis), lax.axis_index(axis), shard.shape[dim])
+    lengths = [n * ways if d == dim else n for d, n in enumerate(shard.shape)]
+    full = lax.dynamic_update_slice_in_dim(
+        jnp.zeros(lengths, shard.dtype), shard, here * lap, axis=dim
+    )
+    going_up = going_down = shard
+    for far in range(1, ways // 2 + 1):
+        going_up = lax.ppermute(going_up, axis, [(d, (d + 1) % ways) for d in range(ways)])
+        full = lax.dynamic_update_slice_in_dim(full, going_up, (here - far) % ways * lap, axis=dim)
+        if 2 * far < ways:
+            going_down = lax.ppermute(going_down, axis, [(d, (d - 1) % ways) for d in range(ways)])
+            full = lax.dynamic_update_slice_in_dim(
+                full, going_down, (here + far) % ways * lap, axis=dim
+            )
+    return full
 
 
 def contract_rows(operand, factor):
@@ -133,7 +151,7 @@
     value_own = projected[:, 2 * model_width :].astype(jnp.bfloat16)
     keys_all, values_all, seq_k, var_k = (
         lax.all_gather(key_own, "col", axis=0, tiled=True),
-        lax.all_gather(value_own, "col", axis=0, tiled=True),
+        gather_around(value_own, "col", 0),
         lax.all_gather(seq_q, "col", axis=0, tiled=True),
         lax.all_gather(var_q, "col", axis=0, tiled=True),
     )

time: 1560 us -> 1580 us (1.013)
  waiting for transfers between devices: 1130 us -> 1080 us
  local copies, waits for them, and re-layouts: 99.4 us -> 132 us
  starting transfers between devices: 17.8 us -> 47.3 us
    all_gather x1, waiting for transfers between devices: 38.1 us -> 0.01 us  [shards(): lax.all_gather(value_own, 'col', axis=0, tiled=True)]
    ppermute x0 -> x15, starting transfers between devices: none -> 30.1 us  [the longest x7 15.3 us: gather_around(): lax.ppermute(going_down, axis, [(d, (d - 1) % ways) for d in range(ways)])]
    ppermute x0 -> x15, waiting for transfers between devices: none -> 22.2 us  [the longest x7 12 us: gather_around(): lax.ppermute(going_down, axis, [(d, (d - 1) % ways) for d in range(ways)])]
    all_gather x1, waiting for transfers between devices: 114 us -> 97.5 us  [shards(): lax.all_gather(w_gate_up, ('row', 'col'), axis=0, tiled=True)]
    unnamed x58 -> x59, local copies, waits for them, and re-layouts: 69.2 us -> 74.7 us
  transfers between devices with their start and end apart: 15 -> 30, of which waited for: 13 -> 18; matrix products, arithmetic and copies ran while one was open for 11% -> 13% of each run, Pallas kernels for 0% -> 0%
where the time goes in v1:
time: 1580 us; the launch traced here: 1570 us
  waiting for transfers between devices  1080 us (68%)
  matrix products  157 us (10%)
  local copies, waits for them, and re-layouts  132 us (8%)
  blocking collectives  124 us (8%)
  starting transfers between devices  47.3 us (3%)
    reduce_scatter x1, waiting for transfers between devices, shards(): lax.psum_scatter(term_gate_up, ('row', 'col'), scatter_dimension=0, tiled...  362 us
    reduce_scatter x1, waiting for transfers between devices, shards(): lax.psum_scatter(term_down, ('row', 'col'), scatter_dimension=0, tiled=True)  187 us
    reduce_scatter x1, waiting for transfers between devices, shards(): lax.psum_scatter(term_qkv, ('row', 'col'), scatter_dimension=0, tiled=True)  163 us
    unnamed x14, waiting for transfers between devices  119 us
    all_gather x1, waiting for transfers between devices, shards(): lax.all_gather(w_gate_up, ('row', 'col'), axis=0, tiled=True)  97.5 us
    unnamed x2, blocking collectives  83 us
    unnamed x59, local copies, waits for them, and re-layouts  74.7 us
    all_gather x1, waiting for transfers between devices, shards(): lax.all_gather(w_down, ('row', 'col'), axis=0, tiled=True)  68.3 us
  transfers between devices with their start and end apart: 30, of which 18 were waited for; matrix products, arithmetic and copies ran while one was open for 13% of the time, Pallas kernels for 0%

profile of v1, /device:TPU:1, one launch (start us, length us, event | category | flops | bytes accessed | tf_op | source)
XLA Modules:
  0.0 1569.8 jit_solution(5466802563144078026)
XLA Ops:
  12.5 7.3 all-to-all-start.1
  21.3 4.6 all-to-all-done.1
  25.9 4.1 all-to-all-start
  31.7 41.9 %all-reduce.5 = (bf16[1024]{0:T(1024)(128)(2,1)S(1)}, bf16[1024]{0:T(1024)(128)(2,1)S(1)}) all-reduce(bf16[1024]{0:T(1024)(128)(2,1)S(1)} %dynamic-update-slice, bf16[1024]{0:T(1024)(128)(2,1)S(1)} %dynamic-update-slice.1), channel_id=1, replica_groups=mesh['row'=2,'col'=16] {'row','col'}, use_global_device_ids=true, to_apply=%add | all-reduce | flops 2048 | bytes 8192
  74.2 11.2 all-gather.9.cloned.1.call-done
  85.3 3.8 fusion.91
  97.1 5.4 collective-permute-done
  102.4 2.9 collective-permute-start.2
  105.3 3.5 collective-permute-done.1
  109.0 2.5 collective-permute-start.4
  111.5 4.6 collective-permute-done.3
  116.6 24.2 %all-gather = s32[16,1,128]{2,1,0:T(1,128)S(1)} all-gather(s32[1,1,128]{2,1,0:T(1,128)S(1)} %reshape.403), channel_id=1, replica_groups=mesh['row'=2,'col'=16] {'col'}, dimensions={0}, use_global_device_ids=true | all-gather | bytes 8704 | tf_op jit(solution)/shard_map/all_gather | solution.py:155
  142.1 17.3 %all-gather.1 = s32[16,1,128]{2,1,0:T(1,128)S(1)} all-gather(s32[1,1,128]{2,1,0:T(1,128)S(1)} %reshape.405), channel_id=1, replica_groups=mesh['row'=2,'col'=16] {'col'}, dimensions={0}, use_global_device_ids=true | all-gather | bytes 8704 | tf_op jit(solution)/shard_map/all_gather | solution.py:156
  162.8 2.5 broadcast_in_dim.143
  170.9 3.2 collective-permute-done.7
  180.0 7.8 collective-permute-start.11
  193.4 5.3 collective-permute-start.13
  200.6 4.1 collective-permute-done.12
  204.7 2.6 collective-permute-start.14
  211.5 7.9 reshape.361
  219.4 5.5 copy.131
  224.9 7.9 reshape.359
  232.8 5.5 copy.129
  238.3 11.6 reshape.415
  249.9 9.8 copy.137
  259.7 32.2 %while.34 = (s32[]{:T(128)}, f32[16,128]{1,0:T(8,128)S(1)}, f32[128,16,64]{0,2,1:T(8,128)S(1)}, s32[16,1,8]{2,0,1:T(8,128)}, s32[2,1024]{1,0:T(2,128)S(1)}, /*in...) while((s32[]{:T(128)}, f32[16,128]{1,0:T(8,128)S(1)}, ...), condition=%wide.wide.region_6.8_spmd.clone, body=%wide.wide.region_4.7_spmd.clone.sunk | while | flops 558368768 | bytes 23127724 | solution.py:183
  260.2 8.7 fusion.161
  268.9 6.7 fusion.162
  276.1 8.7 fusion.161
  284.8 6.9 fusion.162
  294.3 97.5 %all-gather.15.cloned.1.call-done = bf16[1024,8192]{1,0:T(8,128)(2,1)} async-done(((bf16[32,8192]{1,0:T(8,128)(2,1)}), bf16[1024,8192]{1,0:T(8,128)(2,1)}) %all-gather.15.cloned.1.call-update) | async-done | bytes 16777232 | tf_op jit(solution)/shard_map/all_gather | solution.py:137
  391.8 10.2 fusion.99
  402.0 68.3 %all-gather.17.cloned.1.call-done = bf16[4096,1024]{1,0:T(8,128)(2,1)} async-done(((bf16[128,1024]{1,0:T(8,128)(2,1)}), bf16[4096,1024]{1,0:T(8,128)(2,1)}) %all-gather.17.cloned.1.call-update) | async-done | bytes 8388624 | tf_op jit(solution)/shard_map/all_gather | solution.py:138
  470.3 9.1 multiply_convert_fusion.1
  479.5 13.5 multiply_reduce_fusion
  497.4 46.6 %while.35 = (s32[]{:T(128)}, f32[128,16,64]{0,2,1:T(8,128)S(1)}, f32[16]{0:T(128)S(1)}, f32[16]{0:T(128)S(1)}, bf16[2,1024,16,64]{1,3,2,0:T(8,128)(2,1)}, /*inde...) while((s32[]{:T(128)}, f32[128,16,64]{0,2,1:T(8,128)S(1)}, ...), condition=%wide.wide.region_13.15_spmd.clone, body=%wide.wide.region_10.14_spmd.clone.sunk | while | flops 1377304576 | bytes 158108944 | solution.py:274
  498.1 3.1 fusion.172
  501.5 7.2 select_reduce_fusion.5
  508.7 3.9 fusion.173
  512.7 3.0 bitcast_dynamic-update-slice_fusion.6
  516.9 4.1 bitcast_dynamic-update-slice_fusion.7
  521.2 3.1 fusion.172
  524.5 7.2 select_reduce_fusion.5
  531.8 3.9 fusion.173
  535.8 2.9 bitcast_dynamic-update-slice_fusion.6
  539.9 4.1 bitcast_dynamic-update-slice_fusion.7
  544.0 11.0 copy.151
  555.0 11.9 reshape.416
  567.0 11.2 copy.152
  578.2 12.0 reshape.418
  591.2 2.8 fusion.86
  595.0 41.7 %reduce-scatter.19.cloned.1.call-done = bf16[128,1024]{1,0:T(8,128)(2,1)} async-done(((bf16[2048,1024]{1,0:T(8,128)(2,1)}), bf16[128,1024]{1,0:T(8,128)(2,1)}) %reduce-scatter.19.cloned.1.call-update) | async-done | bytes 262160
  637.8 74.6 %reduce-scatter.21.cloned.1.call-done = bf16[128,1024]{1,0:T(8,128)(2,1)} async-done(((bf16[2048,1024]{1,0:T(8,128)(2,1)}), bf16[128,1024]{1,0:T(8,128)(2,1)}) %reduce-scatter.21.cloned.1.call-update) | async-done | bytes 262160
  714.9 6.4 fusion.82
  722.2 8.1 fusion.100
  730.4 14.9 fusion.66
  746.0 5.1 fusion.80
  752.1 5.4 all-to-all-start.2
  757.4 5.4 fusion.68
  762.8 41.1 %all-reduce.4 = (f32[1024]{0:T(1024)S(1)}, f32[1024]{0:T(1024)S(1)}, f32[2,16]{1,0:T(2,128)}) all-reduce(f32[1024]{0:T(1024)S(1)} %get-tuple-element.349, f32[1024]{0:T(1024)S(1)} %copy-done.25, f32[2,16]{1,0:T(2,128)S(1)} %pad_maximum_fusion.10), channel_id=8, replica_groups=mesh['row'=2,'col'=16] {'row','col'}, use_global_device_ids=true, to_apply=%region_22.24.clone | all-reduce | flops 2080 | bytes 16640
  806.4 44.9 %reduce-scatter.13.cloned.1.call-done = f32[32,1024]{1,0:T(8,128)} async-done(((f32[1024,1024]{1,0:T(8,128)}), f32[32,1024]{1,0:T(8,128)}) %reduce-scatter.13.cloned.1.call-update) | async-done | bytes 131088 | tf_op jit(solution)/shard_map/reduce_scatter | solution.py:303
  851.4 162.5 %reduce-scatter.11.cloned.1.call-done = f32[32,3072]{1,0:T(8,128)} async-done(((f32[1024,3072]{1,0:T(8,128)}), f32[32,3072]{1,0:T(8,128)}) %reduce-scatter.11.cloned.1.call-update) | async-done | bytes 393232 | tf_op jit(solution)/shard_map/reduce_scatter | solution.py:302
  1013.9 187.4 %reduce-scatter.17.cloned.1.call-done = f32[128,1024]{1,0:T(8,128)} async-done(((f32[4096,1024]{1,0:T(8,128)}), f32[128,1024]{1,0:T(8,128)}) %reduce-scatter.17.cloned.1.call-update) | async-done | bytes 524304 | tf_op jit(solution)/shard_map/reduce_scatter | solution.py:305
  1201.2 361.5 %reduce-scatter.15.cloned.1.call-done = f32[32,8192]{1,0:T(8,128)} async-done(((f32[1024,8192]{1,0:T(8,128)}), f32[32,8192]{1,0:T(8,128)}) %reduce-scatter.15.cloned.1.call-update) | async-done | bytes 1048592 | tf_op jit(solution)/shard_map/reduce_scatter | solution.py:304
  (249 shorter events, 66.7 us)
Async XLA Ops:
  7.2 12.7 copy-start
  7.2 78.1 %all-gather.9.cloned.1.call-start = ((), (), s32[]{:S(2)}) async-start(), calls=%async_computation.9 | async-start | bytes 6488064 | tf_op jit(solution)/shard_map/all_gather | solution.py:135
  12.5 13.4 all-to-all-start.1
  25.9 48.0 %all-to-all-start = ((bf16[16,8,1024]{2,1,0:T(8,128)(2,1)}), bf16[16,8,1024]{2,1,0:T(8,128)(2,1)S(1)}, u32[]{:S(2)}, u32[]{:S(2)}) async-start(bf16[16,8,1024]{2,1,0:T(8,128)(2,1)} %broadcast_select_fusion.2), calls=%async_computation | async-start | bytes 524288 | tf_op jit(solution)/shard_map/all_to_all | solution.py:127
  29.9 195.0 %all-gather.11.cloned.1.call-start = ((), (), s32[]{:S(2)}) async-start(), calls=%async_computation.10 | async-start | bytes 4456448 | tf_op jit(solution)/shard_map/all_gather | solution.py:153
  73.6 15.6 copy-start.12
  73.9 18.3 %copy-start.16 = (f32[128,32]{0,1:T(8,128)}, f32[128,32]{0,1:T(8,128)S(1)}, u32[]{:S(2)}) copy-start(f32[128,32]{0,1:T(8,128)S(1)} %get-tuple-element.444) | copy-start | bytes 49156
  73.9 18.3 %copy-start.18 = (f32[128,32]{0,1:T(8,128)}, f32[128,32]{0,1:T(8,128)S(1)}, u32[]{:S(2)}) copy-start(f32[128,32]{0,1:T(8,128)S(1)} %get-tuple-element.445) | copy-start | bytes 49156
  74.2 15.0 copy-start.23
  93.1 145.2 %all-gather.19.cloned.1.call-start = ((), (), s32[]{:S(2)}) async-start(), calls=%async_computation.14 | async-start | bytes 4456448 | tf_op jit(solution)/shard_map/all_gather | solution.py:234
  93.9 198.1 %all-gather.13.cloned.1.call-start = ((), (), s32[]{:S(2)}) async-start(), calls=%async_computation.11 | async-start | bytes 2162688 | tf_op jit(solution)/shard_map/all_gather | solution.py:136
  94.5 297.3 %all-gather.15.cloned.1.call-start = ((), (), s32[]{:S(2)}) async-start(), calls=%async_computation.12 | async-start | bytes 17301504 | tf_op jit(solution)/shard_map/all_gather | solution.py:137
  95.1 375.3 %all-gather.17.cloned.1.call-start = ((), (), s32[]{:S(2)}) async-start(), calls=%async_computation.13 | async-start | bytes 8650752 | tf_op jit(solution)/shard_map/all_gather | solution.py:138
  95.6 541.0 %reduce-scatter.19.cloned.1.call-start = ((), (), s32[]{:S(2)}) async-start(), calls=%async_computation.19 | async-start | bytes 4456448
  95.7 6.8 collective-permute-start
  97.1 11.8 collective-permute-start.1
  102.4 6.6 collective-permute-start.2
  108.8 7.2 collective-permute-start.3
  109.0 52.2 %collective-permute-start.4 = (bf16[128,1024]{1,0:T(8,128)(2,1)S(1)}, bf16[128,1024]{1,0:T(8,128)(2,1)S(1)}, u32[]{:S(2)}, u32[]{:S(2)}) collective-permute-start(bf16[128,1024]{1,0:T(8,128)(2,1)S(1)} %collective-permute-done.2), channel_id=1, source_target_pairs={{0,1},{1,2},{2,3},{3,4},{4,5},{5,6},{6,7},{7,8},{8,9},{9,10},{10,1... | collective-permute-start | bytes 786440 | tf_op jit(solution)/shard_map/ppermute | solution.py:21
  116.1 50.2 %collective-permute-start.5 = (bf16[128,1024]{1,0:T(8,128)(2,1)S(1)}, bf16[128,1024]{1,0:T(8,128)(2,1)}, u32[]{:S(2)}, u32[]{:S(2)}) collective-permute-start(bf16[128,1024]{1,0:T(8,128)(2,1)S(1)} %collective-permute-done.3), channel_id=1, source_target_pairs={{0,15},{1,0},{2,1},{3,2},{4,3},{5,4},{6,5},{7,6},{8,7},{9,8},{10,9... | collective-permute-start | bytes 786440 | tf_op jit(solution)/shard_map/ppermute | solution.py:24
  116.1 52.1 %copy-start.21 = (s32[16,1,8]{2,1,0:T(1,128)}, s32[16,1,8]{2,1,0:T(1,128)S(1)}, u32[]{:S(2)}) copy-start(s32[16,1,8]{2,1,0:T(1,128)S(1)} %get-tuple-element.438) | copy-start | bytes 1540
  116.1 52.1 %copy-start.22 = (s32[16,1,8]{2,1,0:T(1,128)}, s32[16,1,8]{2,1,0:T(1,128)S(1)}, u32[]{:S(2)}) copy-start(s32[16,1,8]{2,1,0:T(1,128)S(1)} %get-tuple-element.441) | copy-start | bytes 1540
  161.3 7.0 collective-permute-start.6
  166.3 7.9 collective-permute-start.7
  168.2 10.9 collective-permute-start.8
  174.1 5.9 collective-permute-start.9
  179.1 10.6 collective-permute-start.10
  180.0 13.3 collective-permute-start.11
  189.7 14.9 collective-permute-start.12
  193.4 14.8 collective-permute-start.13
  204.7 5.9 collective-permute-start.14
  249.9 9.8 copy-start.20
  291.9 110.1 %copy-start.8 = (f32[128,16,64]{0,2,1:T(8,128)}, f32[128,16,64]{0,2,1:T(8,128)S(1)}, u32[]{:S(2)}) copy-start(f32[128,16,64]{0,2,1:T(8,128)S(1)} %get-tuple-element.154) | copy-start | bytes 1572868
  292.0 110.0 %copy-start.6 = (bf16[128,16,64]{0,2,1:T(8,128)(2,1)}, bf16[128,16,64]{0,2,1:T(8,128)(2,1)S(1)}, u32[]{:S(2)}) copy-start(bf16[128,16,64]{0,2,1:T(8,128)(2,1)S(1)} %fusion.85) | copy-start | bytes 786436
  391.8 78.5 %copy-start.10 = (bf16[128,1024]{1,0:T(8,128)(2,1)S(1)}, bf16[128,1024]{1,0:T(8,128)(2,1)}, u32[]{:S(2)}) copy-start(bf16[128,1024]{1,0:T(8,128)(2,1)} %param.31) | copy-start | bytes 786436
  493.0 3.6 copy-start.9
  498.1 3.4 copy-start.5
  498.1 3.4 copy-start.14
  501.2 7.5 copy-start.3
  508.7 4.0 copy-start.2
  512.7 4.1 copy-start.4
  512.7 4.1 copy-start.15
  521.1 3.4 copy-start.5
  521.2 3.4 copy-start.14
  524.3 7.5 copy-start.3
  531.8 4.0 copy-start.2
  535.8 4.1 copy-start.4
  535.8 4.1 copy-start.15
  566.9 145.5 %reduce-scatter.21.cloned.1.call-start = ((), (), s32[]{:S(2)}) async-start(), calls=%async_computation.20 | async-start | bytes 4456448
  590.3 0.9 copy-start.7
  590.3 261.1 %reduce-scatter.13.cloned.1.call-start = ((), (), s32[]{:S(2)}) async-start(), calls=%async_computation.16 | async-start | bytes 4325376 | tf_op jit(solution)/shard_map/reduce_scatter | solution.py:303
  594.1 119.6 %copy-start.17 = (f32[128,32]{0,1:T(8,128)S(1)}, f32[128,32]{0,1:T(8,128)}, u32[]{:S(2)}) copy-start(f32[128,32]{0,1:T(8,128)} %copy-done.16) | copy-start | bytes 49156
  594.1 119.6 %copy-start.19 = (f32[128,32]{0,1:T(8,128)S(1)}, f32[128,32]{0,1:T(8,128)}, u32[]{:S(2)}) copy-start(f32[128,32]{0,1:T(8,128)} %copy-done.18) | copy-start | bytes 49156
  594.1 120.8 %copy-start.13 = (f32[1024]{0:T(1024)S(1)}, f32[1024]{0:T(1024)}, u32[]{:S(2)}) copy-start(f32[1024]{0:T(1024)} %copy-done.12) | copy-start | bytes 12292
  594.1 120.8 %copy-start.24 = (f32[128]{0:T(128)S(1)}, f32[128]{0:T(128)}, u32[]{:S(2)}) copy-start(f32[128]{0:T(128)} %copy-done.23) | copy-start | bytes 1540
  594.1 419.8 %reduce-scatter.11.cloned.1.call-start = ((), (), s32[]{:S(2)}) async-start(), calls=%async_computation.15 | async-start | bytes 12976128 | tf_op jit(solution)/shard_map/reduce_scatter | solution.py:302
  721.3 1.0 copy-start.11
  721.3 479.9 %reduce-scatter.17.cloned.1.call-start = ((), (), s32[]{:S(2)}) async-start(), calls=%async_computation.18 | async-start | bytes 17301504 | tf_op jit(solution)/shard_map/reduce_scatter | solution.py:305
  730.4 832.4 %reduce-scatter.15.cloned.1.call-start = ((), (), s32[]{:S(2)}) async-start(), calls=%async_computation.17 | async-start | bytes 34603008 | tf_op jit(solution)/shard_map/reduce_scatter | solution.py:304
  745.3 0.7 copy-start.26
  752.1 53.0 %all-to-all-start.2 = ((bf16[16,8,1024]{2,1,0:T(8,128)(2,1)}), bf16[16,8,1024]{2,1,0:T(8,128)(2,1)S(1)}, u32[]{:S(2)}, u32[]{:S(2)}) async-start(bf16[16,8,1024]{2,1,0:T(8,128)(2,1)} %fusion.84), calls=%async_computation.2 | async-start | bytes 524288 | tf_op jit(solution)/shard_map/all_to_all | solution.py:313
  757.4 5.4 copy-start.25
  757.4 805.3 %copy-start.1 = (bf16[128,1024]{1,0:T(8,128)(2,1)S(1)}, bf16[128,1024]{1,0:T(8,128)(2,1)}, u32[]{:S(2)}) copy-start(bf16[128,1024]{1,0:T(8,128)(2,1)} %param.19) | copy-start | bytes 786436
Sparse Core Ops, SparseCore 0:
  10.9 74.3 all-gather.8
  93.2 59.3 all-gather.10
  155.4 62.4 all-gather.18
  220.6 54.7 all-gather.12
  278.1 113.7 all-gather.14
  394.6 75.7 all-gather.16
  567.1 69.5 reduce-scatter.18
  641.0 71.4 reduce-scatter.20
  715.3 136.0 reduce-scatter.12
  857.8 156.0 reduce-scatter.10
  1016.9 184.3 reduce-scatter.16
  1204.1 358.6 reduce-scatter.14
